TPU v7x, 32 devices: a whole 2x2x4 slice. The times are simulated.
32 devices in a mesh: prow: 8 (over z, y), pcol: 4 (over x, core).
Axes of the slice: x: 2, y: 2, z: 4, core: 2. Of those that a mesh axis runs over, the one named last changes fastest.
Arguments:
- a_panel: float32 [98304, 512], P('prow', 'pcol'), may hold values from -6 to 6
- u_rows: float32 [512, 98304], P('pcol', 'prow'), may hold values from -0.25 to 0.25
- u_col: float32 [98304, 2048], P('prow', 'pcol'), may hold values from -0.01953125 to 0.01953125
- c_in: float32 [98304, 2048], P('prow', 'pcol'), may hold values from -6 to 6
Outputs:
- c_out: float32 [98304, 2048], P('prow', 'pcol')
All inputs are finite; a program needn't handle non-finite values.
Results may differ from a plain program's by a relative error of at most 0.00007.
Values sent between devices are 32-bit elements; how exact they have to be, the bound alone decides.
A program may use at most 192 MiB of HBM per device.

v0:
```python
import functools

import jax
import jax.numpy as jnp
from jax import lax
from jax.experimental import pallas as pl
from jax.experimental.pallas import tpu as pltpu
from jax.sharding import PartitionSpec as P


UNITS = 24
A_CHUNKS = (6, 6, 6, 6)
U_CHUNKS = (6, 6, 5, 3, 2, 2)
TN = (((0,), (0,)), ((), ()))


def parts(x):
    hi = x.astype(jnp.bfloat16)
    return hi, (x - hi.astype(jnp.float32)).astype(jnp.bfloat16)


def dot3(a_hi, a_lo, b_hi, b_lo):
    dot = functools.partial(lax.dot_general, dimension_numbers=TN, preferred_element_type=jnp.float32)
    return dot(a_hi, b_hi) + (dot(a_lo, b_hi) + dot(a_hi, b_lo))


def inner_kernel(first, *refs):
    blocks, (ucol, before, out) = refs[:-3], refs[-3:]

    @pl.when(pl.program_id(0) == 0)
    def _():
        out[...] = jnp.zeros_like(out) if first else before[...]

    u_hi, u_lo = parts(ucol[...])
    width = blocks[0].shape[1]
    for k, block in enumerate(blocks):
        a_hi, a_lo = parts(block[...])
        out[pl.ds(k * width, width), :] += dot3(a_hi, a_lo, u_hi, u_lo)


def update_kernel(*refs):
    blocks, (inner, c_in, _, out, i_hi, i_lo) = refs[:-6], refs[-6:]

    @pl.when(pl.program_id(0) == 0)
    def _():
        i_hi[...], i_lo[...] = parts(inner[...])

    u_hi, u_lo = parts(jnp.concatenate([b[...] for b in blocks], axis=0))
    out[...] = c_in[...] + dot3(u_hi, u_lo, i_hi[...], i_lo[...])


def tile_of(start, size):
    return next(t for t in (1024, 512, 256, 128) if size % t == 0 and start % t == 0)


def add_inner(blocks, ucol, before, start, size):
    tile = tile_of(start, size)
    width, cols = blocks[0][0].shape[1], ucol.shape[1]
    first = before is None
    if first:
        before = jnp.zeros((8, 128), jnp.float32)
    rows = len(blocks) * width
    return pl.pallas_call(
        functools.partial(inner_kernel, first),
        grid=(size // tile,),
        in_specs=[
            pl.BlockSpec((tile, width), lambda i, o=(start - at) // tile: (i + o, 0)) for _, at in blocks
        ] + [
            pl.BlockSpec((tile, cols), lambda i: (i + start // tile, 0)),
            pl.BlockSpec(before.shape, lambda i: (0, 0)),
        ],
        out_specs=pl.BlockSpec((rows, cols), lambda i: (0, 0)),
        out_shape=jax.ShapeDtypeStruct((rows, cols), jnp.float32),
        cost_estimate=pl.CostEstimate(flops=6 * size * rows * cols, bytes_accessed=4 * size * (rows + cols), transcendentals=0),
        name="inner_part",
    )(*[b for b, _ in blocks], ucol, before)


def write_rows(blocks, inner, c_in, out, start, size):
    tile = tile_of(start, size)
    width, (rows, cols) = blocks[0][0].shape[0], inner.shape
    first = out is None
    if first:
        out = jnp.zeros((8, 128), jnp.float32)
    return pl.pallas_call(
        update_kernel,
        grid=(size // tile,),
        in_specs=[
            pl.BlockSpec((width, tile), lambda i, o=(start - at) // tile: (0, i + o)) for _, at in blocks
        ] + [
            pl.BlockSpec((rows, cols), lambda i: (0, 0)),
            pl.BlockSpec((tile, cols), lambda i: (i + start // tile, 0)),
            pl.BlockSpec(memory_space=pl.ANY),
        ],
        out_specs=pl.BlockSpec((tile, cols), lambda i: (i + start // tile, 0)),
        out_shape=jax.ShapeDtypeStruct(c_in.shape, jnp.float32),
        scratch_shapes=[pltpu.VMEM((rows, cols), jnp.bfloat16)] * 2,
        input_output_aliases={} if first else {len(blocks) + 2: 0},
        cost_estimate=pl.CostEstimate(flops=6 * size * rows * cols, bytes_accessed=4 * size * (rows + 2 * cols), transcendentals=0),
        name="update_rows",
    )(*[b for b, _ in blocks], inner, c_in, out)


def sum_over(x, axis, n):
    if n & (n - 1) or x.shape[0] % (8 * n):
        return lax.psum(x, axis)
    me = lax.axis_index(axis)
    bits = [1 << k for k in range(n.bit_length() - 1)]
    swap = lambda y, bit: lax.ppermute(y, axis, [(i, i ^ bit) for i in range(n)])
    for bit in bits:
        up = (me & bit) != 0
        half = x.shape[0] // 2
        low, high = x[:half], x[half:]
        x = jnp.where(up, high, low) + swap(jnp.where(up, low, high), bit)
    for bit in bits[::-1]:
        up = (me & bit) != 0
        other = swap(x, bit)
        x = jnp.concatenate([jnp.where(up, other, x), jnp.where(up, x, other)], axis=0)
    return x


def ranges(units, unit):
    start = 0
    for n in units:
        yield start, n * unit
        start += n * unit


def paired(n_row, a, u, ucol, c_in):
    unit = a.shape[0] // UNITS
    over_core = lambda x: lax.ppermute(x, "pcol", [(i, i ^ 1) for i in range(4)])
    over_chip = lambda x: lax.ppermute(x, "pcol", [(i, i ^ 2) for i in range(4)])

    a_ranges, u_ranges = list(ranges(A_CHUNKS, unit)), list(ranges(U_CHUNKS, unit))
    head = lax.slice_in_dim(a, 0, a_ranges[0][1], axis=0)
    head, a_rest, u_rest = lax.optimization_barrier((head, a, u))
    far_a = [over_chip(head)]
    for k, (r, n) in enumerate(a_ranges[1:], 1):
        far_a.append(over_chip(lax.slice_in_dim(a_rest, r, r + n, axis=0)))
    far_u = [over_chip(lax.slice_in_dim(u_rest, r, r + n, axis=1)) for r, n in u_ranges]

    a_core = over_core(a)
    inner = None
    for k, (r, n) in enumerate(a_ranges):
        xc = over_core(far_a[k])
        inner = add_inner([(a, 0), (a_core, 0), (far_a[k], r), (xc, r)], ucol, inner, r, n)
    u_core = over_core(u)
    inner = sum_over(inner, "prow", n_row)
    out = None
    for k, (r, n) in enumerate(u_ranges):
        xc = over_core(far_u[k])
        out = write_rows([(u, 0), (u_core, 0), (far_u[k], r), (xc, r)], inner, c_in, out, r, n)
    return out


def gathered(a, u, ucol, c_in):
    a_full = lax.all_gather(a, "pcol", axis=1, tiled=True)
    u_full = lax.all_gather(u, "pcol", axis=0, tiled=True)
    dot = functools.partial(jnp.dot, precision=lax.Precision.HIGHEST, preferred_element_type=jnp.float32)
    inner = lax.psum(dot(a_full.T, ucol), "prow")
    return c_in + dot(u_full.T, inner)


def solution(mesh):
    n_row, n_col = mesh.shape["prow"], mesh.shape["pcol"]
    two_chips = n_col == 4

    def on_device(a, u, ucol, c_in):
        if two_chips and a.shape[0] % (128 * UNITS) == 0 and a.shape[1] % 128 == 0:
            return paired(n_row, a, u, ucol, c_in)
        return gathered(a, u, ucol, c_in)

    placed = (P("prow", "pcol"), P("pcol", "prow"), P("prow", "pcol"), P("prow", "pcol"))
    return jax.shard_map(
        on_device, mesh=mesh, in_specs=placed, out_specs=P("prow", "pcol"), check_vma=False
    )
```

profile of v0, /device:TPU:0, one launch (start us, length us, event | category | flops | bytes accessed | tf_op | source)
XLA Modules:
  0.0 387.0 jit_solution(15359104435373370042)
XLA Ops:
  9.4 30.4 %collective-permute-done.10.refs_2_ = f32[3072,128]{1,0:T(8,128)S(1)} collective-permute-done((f32[3072,128]{1,0:T(8,128)S(1)}, f32[3072,128]{1,0:T(8,128)S(1)}, u32[]{:S(2)}, u32[]{:S(2)}) %collective-permute-start.10) | collective-permute-done | bytes 1572896 | tf_op jit(solution)/shard_map/ppermute | solution.py:132
  39.8 33.8 %collective-permute-done.8.refs_2_ = f32[3072,128]{1,0:T(8,128)} collective-permute-done((f32[3072,128]{1,0:T(8,128)S(1)}, f32[3072,128]{1,0:T(8,128)}, u32[]{:S(2)}, u32[]{:S(2)}) %collective-permute-start.8) | collective-permute-done | bytes 1572896 | tf_op jit(solution)/shard_map/ppermute | solution.py:132
  73.6 33.7 %collective-permute-done.6.refs_2_ = f32[3072,128]{1,0:T(8,128)} collective-permute-done((f32[3072,128]{1,0:T(8,128)S(1)}, f32[3072,128]{1,0:T(8,128)}, u32[]{:S(2)}, u32[]{:S(2)}) %collective-permute-start.6) | collective-permute-done | bytes 1572896 | tf_op jit(solution)/shard_map/ppermute | solution.py:132
  107.3 33.5 %collective-permute-done.4.refs_2_ = f32[3072,128]{1,0:T(8,128)} collective-permute-done((f32[3072,128]{1,0:T(8,128)S(1)}, f32[3072,128]{1,0:T(8,128)}, u32[]{:S(2)}, u32[]{:S(2)}) %collective-permute-start.4) | collective-permute-done | bytes 1572896 | tf_op jit(solution)/shard_map/ppermute | solution.py:132
  142.0 9.7 %inner_part.4.refs_5_ = f32[512,512]{1,0:T(8,128)} custom-call(f32[12288,128]{1,0:T(8,128)} %refs_0_.13, f32[12288,128]{1,0:T(8,128)} %collective-permute-done.3.refs_1_, f32[3072,128]{1,0:T(8,128)} %copy-done.1, f32[3072,128]{1,0:T(8,128)} %copy-done.2, f32[12288,512]{1,0:T(8,128)} %refs_4_.7, f32[8,128]{1,0:T(8,128)} %broadcast_1_refs_5__refs_6_.2.refs_5_.refs_6_), custom_call_target="tpu_custom_call" | custom-call | flops 4831838208 | bytes 12582912 | tf_op jit(solution)/shard_map/inner_part/pallas_call | solution.py:63
  151.7 10.4 %inner_part.5.refs_5_ = f32[512,512]{1,0:T(8,128)} custom-call(f32[12288,128]{1,0:T(8,128)} %refs_0_.13, f32[12288,128]{1,0:T(8,128)} %collective-permute-done.3.refs_1_, f32[3072,128]{1,0:T(8,128)} %collective-permute-done.8.refs_2_, f32[3072,128]{1,0:T(8,128)} %collective-permute-done.9.refs_3_, f32[12288,512]{1,0:T(8,128)} %refs_4_.7, ...), custom_call_target="tpu_custom_call" | custom-call | flops 4831838208 | bytes 12582912 | tf_op jit(solution)/shard_map/inner_part/pallas_call | solution.py:63
  162.1 10.4 %inner_part.6.refs_5_ = f32[512,512]{1,0:T(8,128)} custom-call(f32[12288,128]{1,0:T(8,128)} %refs_0_.13, f32[12288,128]{1,0:T(8,128)} %collective-permute-done.3.refs_1_, f32[3072,128]{1,0:T(8,128)} %collective-permute-done.6.refs_2_, f32[3072,128]{1,0:T(8,128)} %collective-permute-done.7.refs_3_, f32[12288,512]{1,0:T(8,128)} %refs_4_.7, ...), custom_call_target="tpu_custom_call" | custom-call | flops 4831838208 | bytes 12582912 | tf_op jit(solution)/shard_map/inner_part/pallas_call | solution.py:63
  172.5 10.4 %inner_part.7 = f32[512,512]{1,0:T(8,128)} custom-call(f32[12288,128]{1,0:T(8,128)} %refs_0_.13, f32[12288,128]{1,0:T(8,128)} %collective-permute-done.3.refs_1_, f32[3072,128]{1,0:T(8,128)} %collective-permute-done.4.refs_2_, f32[3072,128]{1,0:T(8,128)} %collective-permute-done.5.refs_3_, f32[12288,512]{1,0:T(8,128)} %refs_4_.7, f32[512,512]{1,0:T(8,128)} %inner_part.6.refs_5_), custom_call_target="tpu_custom_call" | custom-call | flops 4831838208 | bytes 12582912 | tf_op jit(solution)/shard_map/inner_part/pallas_call | solution.py:63
  186.0 3.3 fusion
  190.8 7.9 %collective-permute-done.12 = f32[256,512]{1,0:T(8,128)} collective-permute-done((f32[256,512]{1,0:T(8,128)S(1)}, f32[256,512]{1,0:T(8,128)}, u32[]{:S(2)}, u32[]{:S(2)}) %collective-permute-start.12) | collective-permute-done | bytes 524320 | tf_op jit(solution)/shard_map/ppermute | solution.py:109
  212.1 4.1 %collective-permute-done.14 = f32[64,512]{1,0:T(8,128)S(1)} collective-permute-done((f32[64,512]{1,0:T(8,128)S(1)}, f32[64,512]{1,0:T(8,128)S(1)}, u32[]{:S(2)}, u32[]{:S(2)}) %collective-permute-start.14) | collective-permute-done | bytes 131104 | tf_op jit(solution)/shard_map/ppermute | solution.py:109
  217.7 9.2 %collective-permute-done.26.refs_2_ = f32[128,3072]{1,0:T(8,128)} collective-permute-done((f32[128,3072]{1,0:T(8,128)}, f32[128,3072]{1,0:T(8,128)}, u32[]{:S(2)}, u32[]{:S(2)}) %collective-permute-start.26) | collective-permute-done | bytes 1572896 | tf_op jit(solution)/shard_map/ppermute | solution.py:132
  229.5 5.1 %collective-permute-done.15 = f32[64,512]{1,0:T(8,128)S(1)} collective-permute-done((f32[64,512]{1,0:T(8,128)S(1)}, f32[64,512]{1,0:T(8,128)S(1)}, u32[]{:S(2)}, u32[]{:S(2)}) %collective-permute-start.15) | collective-permute-done | bytes 131104 | tf_op jit(solution)/shard_map/ppermute | solution.py:109
  234.6 64.5 %collective-permute-done.18.refs_2_ = f32[128,1024]{1,0:T(8,128)} collective-permute-done((f32[128,1024]{1,0:T(8,128)S(1)}, f32[128,1024]{1,0:T(8,128)}, u32[]{:S(2)}, u32[]{:S(2)}) %collective-permute-start.18) | collective-permute-done | bytes 524320 | tf_op jit(solution)/shard_map/ppermute | solution.py:132
  302.2 4.5 %collective-permute-done.16 = f32[128,512]{1,0:T(8,128)S(1)} collective-permute-done((f32[128,512]{1,0:T(8,128)S(1)}, f32[128,512]{1,0:T(8,128)S(1)}, u32[]{:S(2)}, u32[]{:S(2)}) %collective-permute-start.16) | collective-permute-done | bytes 262176 | tf_op jit(solution)/shard_map/ppermute | solution.py:109
  306.8 7.0 %collective-permute-done.1.refs_2_ = f32[128,1024]{1,0:T(8,128)} collective-permute-done((f32[128,1024]{1,0:T(8,128)S(1)}, f32[128,1024]{1,0:T(8,128)}, u32[]{:S(2)}, u32[]{:S(2)}) %collective-permute-start.1) | collective-permute-done | bytes 524320 | tf_op jit(solution)/shard_map/ppermute | solution.py:132
  317.1 8.8 %collective-permute-done.17 = f32[256,512]{1,0:T(8,128)S(1)} collective-permute-done((f32[256,512]{1,0:T(8,128)S(1)}, f32[256,512]{1,0:T(8,128)S(1)}, u32[]{:S(2)}, u32[]{:S(2)}) %collective-permute-start.17) | collective-permute-done | bytes 524320 | tf_op jit(solution)/shard_map/ppermute | solution.py:109
  327.0 6.2 %collective-permute-done.20.refs_2_ = f32[128,1536]{1,0:T(8,128)} collective-permute-done((f32[128,1536]{1,0:T(8,128)S(1)}, f32[128,1536]{1,0:T(8,128)}, u32[]{:S(2)}, u32[]{:S(2)}) %collective-permute-start.20) | collective-permute-done | bytes 786464 | tf_op jit(solution)/shard_map/ppermute | solution.py:132
  334.3 11.5 %update_rows.6.refs_6_ = f32[12288,512]{1,0:T(8,128)} custom-call(f32[128,12288]{1,0:T(8,128)} %refs_0_.19, f32[128,12288]{1,0:T(8,128)} %collective-permute-done.refs_1_, f32[128,3072]{1,0:T(8,128)} %collective-permute-done.26.refs_2_, f32[128,3072]{1,0:T(8,128)} %copy-done.3, f32[512,512]{1,0:T(8,128)} %pad_maximum_fusion.refs_4_, f32[12288,512]{1,0:T(8,128)} %refs_5_.11, ...), custom_call_target="tpu_custom_call" | custom-call | flops 4831838208 | bytes 18874368 | tf_op jit(solution)/shard_map/update_rows/pallas_call | solution.py:85
  347.0 11.3 %update_rows.7.refs_6_ = f32[12288,512]{1,0:T(8,128)} custom-call(f32[128,12288]{1,0:T(8,128)} %refs_0_.19, f32[128,12288]{1,0:T(8,128)} %collective-permute-done.refs_1_, f32[128,3072]{1,0:T(8,128)} %collective-permute-done.24.refs_2_, f32[128,3072]{1,0:T(8,128)} %copy-done.4, f32[512,512]{1,0:T(8,128)} %pad_maximum_fusion.refs_4_, ...), custom_call_target="tpu_custom_call", output_to_operand_aliasing={{}: (6, {})} | custom-call | flops 4831838208 | bytes 18874368 | tf_op jit(solution)/shard_map/update_rows/pallas_call | solution.py:85
  358.3 10.1 %update_rows.8.refs_6_ = f32[12288,512]{1,0:T(8,128)} custom-call(f32[128,12288]{1,0:T(8,128)} %refs_0_.19, f32[128,12288]{1,0:T(8,128)} %collective-permute-done.refs_1_, f32[128,2560]{1,0:T(8,128)} %collective-permute-done.22.refs_2_, f32[128,2560]{1,0:T(8,128)} %collective-permute-done.23.refs_3_, ...), custom_call_target="tpu_custom_call", output_to_operand_aliasing={{}: (6, {})} | custom-call | flops 4026531840 | bytes 15728640 | tf_op jit(solution)/shard_map/update_rows/pallas_call | solution.py:85
  368.4 7.1 %update_rows.9.refs_6_ = f32[12288,512]{1,0:T(8,128)} custom-call(f32[128,12288]{1,0:T(8,128)} %refs_0_.19, f32[128,12288]{1,0:T(8,128)} %collective-permute-done.refs_1_, f32[128,1536]{1,0:T(8,128)} %collective-permute-done.20.refs_2_, f32[128,1536]{1,0:T(8,128)} %collective-permute-done.21.refs_3_, ...), custom_call_target="tpu_custom_call", output_to_operand_aliasing={{}: (6, {})} | custom-call | flops 2415919104 | bytes 9437184 | tf_op jit(solution)/shard_map/update_rows/pallas_call | solution.py:85
  375.6 5.7 %update_rows.10.refs_6_ = f32[12288,512]{1,0:T(8,128)} custom-call(f32[128,12288]{1,0:T(8,128)} %refs_0_.19, f32[128,12288]{1,0:T(8,128)} %collective-permute-done.refs_1_, f32[128,1024]{1,0:T(8,128)} %collective-permute-done.18.refs_2_, f32[128,1024]{1,0:T(8,128)} %collective-permute-done.19.refs_3_, ...), custom_call_target="tpu_custom_call", output_to_operand_aliasing={{}: (6, {})} | custom-call | flops 1610612736 | bytes 6291456 | tf_op jit(solution)/shard_map/update_rows/pallas_call | solution.py:85
  381.3 5.7 %update_rows.11 = f32[12288,512]{1,0:T(8,128)} custom-call(f32[128,12288]{1,0:T(8,128)} %refs_0_.19, f32[128,12288]{1,0:T(8,128)} %collective-permute-done.refs_1_, f32[128,1024]{1,0:T(8,128)} %collective-permute-done.1.refs_2_, f32[128,1024]{1,0:T(8,128)} %collective-permute-done.2.refs_3_, ...), custom_call_target="tpu_custom_call", output_to_operand_aliasing={{}: (6, {})} | custom-call | flops 1610612736 | bytes 6291456 | tf_op jit(solution)/shard_map/update_rows/pallas_call | solution.py:85
  (71 shorter events, 42.7 us)
Async XLA Ops:
  0.0 141.4 %collective-permute-start.3 = (f32[12288,128]{1,0:T(8,128)}, f32[12288,128]{1,0:T(8,128)}, u32[]{:S(2)}, u32[]{:S(2)}) collective-permute-start(f32[12288,128]{1,0:T(8,128)} %refs_0_.13), channel_id=1, source_target_pairs={{0,1},{1,0},{2,3},{3,2},{4,5},{5,4},{6,7},{7,6},{8,9},{9,8},{10,11... | collective-permute-start | bytes 18874376 | tf_op jit(solution)/shard_map/ppermute | solution.py:131
  2.0 37.8 %collective-permute-start.10 = (f32[3072,128]{1,0:T(8,128)S(1)}, f32[3072,128]{1,0:T(8,128)S(1)}, u32[]{:S(2)}, u32[]{:S(2)}) collective-permute-start(f32[3072,128]{1,0:T(8,128)S(1)} %slice.48), channel_id=1, source_target_pairs={{0,2},{1,3},{2,0},{3,1},{4,6},{5,7},{6,4},{7,5},{8,10},{9,11},{10,... | collective-permute-start | bytes 4718600 | tf_op jit(solution)/shard_map/ppermute | solution.py:132
  7.2 66.4 %collective-permute-start.8 = (f32[3072,128]{1,0:T(8,128)S(1)}, f32[3072,128]{1,0:T(8,128)}, u32[]{:S(2)}, u32[]{:S(2)}) collective-permute-start(f32[3072,128]{1,0:T(8,128)S(1)} %get-tuple-element.15), channel_id=1, source_target_pairs={{0,2},{1,3},{2,0},{3,1},{4,6},{5,7},{6,4},{7,5},{8,10},{9,11},{10,... | collective-permute-start | bytes 4718600 | tf_op jit(solution)/shard_map/ppermute | solution.py:132
  7.3 100.0 %collective-permute-start.6 = (f32[3072,128]{1,0:T(8,128)S(1)}, f32[3072,128]{1,0:T(8,128)}, u32[]{:S(2)}, u32[]{:S(2)}) collective-permute-start(f32[3072,128]{1,0:T(8,128)S(1)} %get-tuple-element.16), channel_id=1, source_target_pairs={{0,2},{1,3},{2,0},{3,1},{4,6},{5,7},{6,4},{7,5},{8,10},{9,11},{10,... | collective-permute-start | bytes 4718600 | tf_op jit(solution)/shard_map/ppermute | solution.py:132
  9.3 131.5 %collective-permute-start.4 = (f32[3072,128]{1,0:T(8,128)S(1)}, f32[3072,128]{1,0:T(8,128)}, u32[]{:S(2)}, u32[]{:S(2)}) collective-permute-start(f32[3072,128]{1,0:T(8,128)S(1)} %get-tuple-element.17), channel_id=1, source_target_pairs={{0,2},{1,3},{2,0},{3,1},{4,6},{5,7},{6,4},{7,5},{8,10},{9,11},{10,... | collective-permute-start | bytes 4718600 | tf_op jit(solution)/shard_map/ppermute | solution.py:132
  39.8 101.0 %collective-permute-start.11 = (f32[3072,128]{1,0:T(8,128)S(1)}, f32[3072,128]{1,0:T(8,128)S(1)}, u32[]{:S(2)}, u32[]{:S(2)}) collective-permute-start(f32[3072,128]{1,0:T(8,128)S(1)} %collective-permute-done.10.refs_2_), channel_id=1, source_target_pairs={{0,1},{1,0},{2,3},{3,2},{4,5},{5,4},{6,7},{7,6},{8,9},{9,8},{10,11... | collective-permute-start | bytes 4718600 | tf_op jit(solution)/shard_map/ppermute | solution.py:131
  73.6 78.1 %collective-permute-start.9 = (f32[3072,128]{1,0:T(8,128)}, f32[3072,128]{1,0:T(8,128)}, u32[]{:S(2)}, u32[]{:S(2)}) collective-permute-start(f32[3072,128]{1,0:T(8,128)} %collective-permute-done.8.refs_2_), channel_id=1, source_target_pairs={{0,1},{1,0},{2,3},{3,2},{4,5},{5,4},{6,7},{7,6},{8,9},{9,8},{10,11... | collective-permute-start | bytes 4718600 | tf_op jit(solution)/shard_map/ppermute | solution.py:131
  107.3 54.8 %collective-permute-start.7 = (f32[3072,128]{1,0:T(8,128)}, f32[3072,128]{1,0:T(8,128)}, u32[]{:S(2)}, u32[]{:S(2)}) collective-permute-start(f32[3072,128]{1,0:T(8,128)} %collective-permute-done.6.refs_2_), channel_id=1, source_target_pairs={{0,1},{1,0},{2,3},{3,2},{4,5},{5,4},{6,7},{7,6},{8,9},{9,8},{10,11... | collective-permute-start | bytes 4718600 | tf_op jit(solution)/shard_map/ppermute | solution.py:131
  140.8 31.6 %collective-permute-start.5 = (f32[3072,128]{1,0:T(8,128)}, f32[3072,128]{1,0:T(8,128)}, u32[]{:S(2)}, u32[]{:S(2)}) collective-permute-start(f32[3072,128]{1,0:T(8,128)} %collective-permute-done.4.refs_2_), channel_id=1, source_target_pairs={{0,1},{1,0},{2,3},{3,2},{4,5},{5,4},{6,7},{7,6},{8,9},{9,8},{10,11... | collective-permute-start | bytes 4718600 | tf_op jit(solution)/shard_map/ppermute | solution.py:131
  140.8 192.9 %collective-permute-start = (f32[128,12288]{1,0:T(8,128)}, f32[128,12288]{1,0:T(8,128)}, u32[]{:S(2)}, u32[]{:S(2)}) collective-permute-start(f32[128,12288]{1,0:T(8,128)} %refs_0_.19), channel_id=1, source_target_pairs={{0,1},{1,0},{2,3},{3,2},{4,5},{5,4},{6,7},{7,6},{8,9},{9,8},{10,11... | collective-permute-start | bytes 18874376 | tf_op jit(solution)/shard_map/ppermute | solution.py:131
  184.2 14.5 %collective-permute-start.12 = (f32[256,512]{1,0:T(8,128)S(1)}, f32[256,512]{1,0:T(8,128)}, u32[]{:S(2)}, u32[]{:S(2)}) collective-permute-start(f32[256,512]{1,0:T(8,128)S(1)} %slice_select_fusion), channel_id=1, source_target_pairs={{0,4},{4,0},{8,12},{12,8},{16,20},{20,16},{24,28},{28,24},{1,5},{5... | collective-permute-start | bytes 1572872 | tf_op jit(solution)/shard_map/ppermute | solution.py:109
  189.3 37.6 %collective-permute-start.26 = (f32[128,3072]{1,0:T(8,128)}, f32[128,3072]{1,0:T(8,128)}, u32[]{:S(2)}, u32[]{:S(2)}) collective-permute-start(f32[128,3072]{1,0:T(8,128)} %get-tuple-element.11), channel_id=1, source_target_pairs={{0,2},{1,3},{2,0},{3,1},{4,6},{5,7},{6,4},{7,5},{8,10},{9,11},{10,... | collective-permute-start | bytes 4718600 | tf_op jit(solution)/shard_map/ppermute | solution.py:132
  201.8 99.0 %collective-permute-start.24 = (f32[128,3072]{1,0:T(8,128)S(1)}, f32[128,3072]{1,0:T(8,128)}, u32[]{:S(2)}, u32[]{:S(2)}) collective-permute-start(f32[128,3072]{1,0:T(8,128)S(1)} %get-tuple-element.12), channel_id=1, source_target_pairs={{0,2},{1,3},{2,0},{3,1},{4,6},{5,7},{6,4},{7,5},{8,10},{9,11},{10,... | collective-permute-start | bytes 4718600 | tf_op jit(solution)/shard_map/ppermute | solution.py:132
  205.7 109.8 %collective-permute-start.22 = (f32[128,2560]{1,0:T(8,128)}, f32[128,2560]{1,0:T(8,128)}, u32[]{:S(2)}, u32[]{:S(2)}) collective-permute-start(f32[128,2560]{1,0:T(8,128)} %slice.61), channel_id=1, source_target_pairs={{0,2},{1,3},{2,0},{3,1},{4,6},{5,7},{6,4},{7,5},{8,10},{9,11},{10,... | collective-permute-start | bytes 3932168 | tf_op jit(solution)/shard_map/ppermute | solution.py:132
  216.2 83.0 %collective-permute-start.18 = (f32[128,1024]{1,0:T(8,128)S(1)}, f32[128,1024]{1,0:T(8,128)}, u32[]{:S(2)}, u32[]{:S(2)}) collective-permute-start(f32[128,1024]{1,0:T(8,128)S(1)} %get-tuple-element.13), channel_id=1, source_target_pairs={{0,2},{1,3},{2,0},{3,1},{4,6},{5,7},{6,4},{7,5},{8,10},{9,11},{10,... | collective-permute-start | bytes 1572872 | tf_op jit(solution)/shard_map/ppermute | solution.py:132
  234.6 98.6 %collective-permute-start.27 = (f32[128,3072]{1,0:T(8,128)}, f32[128,3072]{1,0:T(8,128)S(1)}, u32[]{:S(2)}, u32[]{:S(2)}) collective-permute-start(f32[128,3072]{1,0:T(8,128)} %collective-permute-done.26.refs_2_), channel_id=1, source_target_pairs={{0,1},{1,0},{2,3},{3,2},{4,5},{5,4},{6,7},{7,6},{8,9},{9,8},{10,11... | collective-permute-start | bytes 4718600 | tf_op jit(solution)/shard_map/ppermute | solution.py:131
  300.8 13.0 %collective-permute-start.1 = (f32[128,1024]{1,0:T(8,128)S(1)}, f32[128,1024]{1,0:T(8,128)}, u32[]{:S(2)}, u32[]{:S(2)}) collective-permute-start(f32[128,1024]{1,0:T(8,128)S(1)} %get-tuple-element.14), channel_id=1, source_target_pairs={{0,2},{1,3},{2,0},{3,1},{4,6},{5,7},{6,4},{7,5},{8,10},{9,11},{10,... | collective-permute-start | bytes 1572872 | tf_op jit(solution)/shard_map/ppermute | solution.py:132
  306.7 39.1 %collective-permute-start.25 = (f32[128,3072]{1,0:T(8,128)}, f32[128,3072]{1,0:T(8,128)S(1)}, u32[]{:S(2)}, u32[]{:S(2)}) collective-permute-start(f32[128,3072]{1,0:T(8,128)} %collective-permute-done.24.refs_2_), channel_id=1, source_target_pairs={{0,1},{1,0},{2,3},{3,2},{4,5},{5,4},{6,7},{7,6},{8,9},{9,8},{10,11... | collective-permute-start | bytes 4718600 | tf_op jit(solution)/shard_map/ppermute | solution.py:131
  313.8 12.1 %collective-permute-start.17 = (f32[256,512]{1,0:T(8,128)S(1)}, f32[256,512]{1,0:T(8,128)S(1)}, u32[]{:S(2)}, u32[]{:S(2)}) collective-permute-start(f32[256,512]{1,0:T(8,128)S(1)} %pad_maximum_fusion.1), channel_id=1, source_target_pairs={{0,4},{4,0},{8,12},{12,8},{16,20},{20,16},{24,28},{28,24},{1,5},{5... | collective-permute-start | bytes 1572872 | tf_op jit(solution)/shard_map/ppermute | solution.py:109
  315.6 17.6 %collective-permute-start.20 = (f32[128,1536]{1,0:T(8,128)S(1)}, f32[128,1536]{1,0:T(8,128)}, u32[]{:S(2)}, u32[]{:S(2)}) collective-permute-start(f32[128,1536]{1,0:T(8,128)S(1)} %slice.60), channel_id=1, source_target_pairs={{0,2},{1,3},{2,0},{3,1},{4,6},{5,7},{6,4},{7,5},{8,10},{9,11},{10,... | collective-permute-start | bytes 2359304 | tf_op jit(solution)/shard_map/ppermute | solution.py:132
  325.8 32.4 %collective-permute-start.23 = (f32[128,2560]{1,0:T(8,128)}, f32[128,2560]{1,0:T(8,128)}, u32[]{:S(2)}, u32[]{:S(2)}) collective-permute-start(f32[128,2560]{1,0:T(8,128)} %collective-permute-done.22.refs_2_), channel_id=1, source_target_pairs={{0,1},{1,0},{2,3},{3,2},{4,5},{5,4},{6,7},{7,6},{8,9},{9,8},{10,11... | collective-permute-start | bytes 3932168 | tf_op jit(solution)/shard_map/ppermute | solution.py:131
  333.2 42.4 %collective-permute-start.19 = (f32[128,1024]{1,0:T(8,128)}, f32[128,1024]{1,0:T(8,128)}, u32[]{:S(2)}, u32[]{:S(2)}) collective-permute-start(f32[128,1024]{1,0:T(8,128)} %collective-permute-done.18.refs_2_), channel_id=1, source_target_pairs={{0,1},{1,0},{2,3},{3,2},{4,5},{5,4},{6,7},{7,6},{8,9},{9,8},{10,11... | collective-permute-start | bytes 1572872 | tf_op jit(solution)/shard_map/ppermute | solution.py:131
  333.2 48.1 %collective-permute-start.2 = (f32[128,1024]{1,0:T(8,128)}, f32[128,1024]{1,0:T(8,128)}, u32[]{:S(2)}, u32[]{:S(2)}) collective-permute-start(f32[128,1024]{1,0:T(8,128)} %collective-permute-done.1.refs_2_), channel_id=1, source_target_pairs={{0,1},{1,0},{2,3},{3,2},{4,5},{5,4},{6,7},{7,6},{8,9},{9,8},{10,11... | collective-permute-start | bytes 1572872 | tf_op jit(solution)/shard_map/ppermute | solution.py:131
  333.7 34.7 %collective-permute-start.21 = (f32[128,1536]{1,0:T(8,128)}, f32[128,1536]{1,0:T(8,128)}, u32[]{:S(2)}, u32[]{:S(2)}) collective-permute-start(f32[128,1536]{1,0:T(8,128)} %collective-permute-done.20.refs_2_), channel_id=1, source_target_pairs={{0,1},{1,0},{2,3},{3,2},{4,5},{5,4},{6,7},{7,6},{8,9},{9,8},{10,11... | collective-permute-start | bytes 2359304 | tf_op jit(solution)/shard_map/ppermute | solution.py:131
  (9 other events, 151.7 us)
where the time goes:
time: 388 us; the launch traced here: 387 us
  waiting for transfers between devices  250 us (64%)
  Pallas kernels  92.2 us (24%)
  starting transfers between devices  25.5 us (7%)
  local copies, waits for them, and re-layouts  14.9 us (4%)
  other arithmetic  3.88 us (1%)
    ppermute x10, waiting for transfers between devices, paired(): lax.ppermute(x, 'pcol', [(i, i ^ 2) for i in range(4)])  218 us
    pallas_call x6, Pallas kernels, write_rows(): pl.pallas_call(update_kernel, grid=(size // tile,), in_specs=[pl.BlockSpe...  51.4 us
    pallas_call x4, Pallas kernels, add_inner(): pl.pallas_call(functools.partial(inner_kernel, first), grid=(size // tile...  40.8 us
    ppermute x6, waiting for transfers between devices, sum_over(): lax.ppermute(y, axis, [(i, i ^ bit) for i in range(n)])  32 us
    ppermute x10, starting transfers between devices, paired(): lax.ppermute(x, 'pcol', [(i, i ^ 2) for i in range(4)])  12.7 us
    ppermute x6, starting transfers between devices, sum_over(): lax.ppermute(y, axis, [(i, i ^ bit) for i in range(n)])  11.2 us
    slice x4, local copies, waits for them, and re-layouts, paired(): lax.slice_in_dim(u_rest, r, r + n, axis=1)  8.25 us
  transfers between devices with their start and end apart: 28, of which 14 were waited for; matrix products, arithmetic and copies ran while one was open for 4% of the time, Pallas kernels for 22%

commit v1 on v0

--- a/solution.py
+++ b/solution.py
@@ -9,8 +9,8 @@
 
 
 UNITS = 24
-A_CHUNKS = (6, 6, 6, 6)
-U_CHUNKS = (6, 6, 5, 3, 2, 2)
+A_CHUNKS = (1, 5, 6, 6, 4, 2)
+U_CHUNKS = (6, 6, 5, 4, 2, 1)
 TN = (((0,), (0,)), ((), ()))
 
 
@@ -50,7 +50,8 @@
 
 
 def tile_of(start, size):
-    return next(t for t in (1024, 512, 256, 128) if size % t == 0 and start % t == 0)
+    sizes = (512, 256, 128) if size > 1024 else (256, 128)
+    return next(t for t in sizes if size % t == 0 and start % t == 0)
 
 
 def add_inner(blocks, ucol, before, start, size):
@@ -132,11 +133,12 @@
     over_chip = lambda x: lax.ppermute(x, "pcol", [(i, i ^ 2) for i in range(4)])
 
     a_ranges, u_ranges = list(ranges(A_CHUNKS, unit)), list(ranges(U_CHUNKS, unit))
-    head = lax.slice_in_dim(a, 0, a_ranges[0][1], axis=0)
-    head, a_rest, u_rest = lax.optimization_barrier((head, a, u))
-    far_a = [over_chip(head)]
-    for k, (r, n) in enumerate(a_ranges[1:], 1):
-        far_a.append(over_chip(lax.slice_in_dim(a_rest, r, r + n, axis=0)))
+    far_a, a_rest, u_rest = [], a, u
+    for k, (r, n) in enumerate(a_ranges):
+        piece = lax.slice_in_dim(a_rest, r, r + n, axis=0)
+        if k < 2:
+            piece, a_rest, u_rest = lax.optimization_barrier((piece, a_rest, u_rest))
+        far_a.append(over_chip(piece))
     far_u = [over_chip(lax.slice_in_dim(u_rest, r, r + n, axis=1)) for r, n in u_ranges]
 
     a_core = over_core(a)

time: 388 us -> 399 us (1.028)
  Pallas kernels: 92.2 us -> 100 us
  waiting for transfers between devices: 250 us -> 244 us
  local copies, waits for them, and re-layouts: 14.9 us -> 19.9 us
    ppermute x10 -> x12, waiting for transfers between devices: 218 us -> 207 us  [paired(): lax.ppermute(x, 'pcol', [(i, i ^ 2) for i in range(4)])]
    pallas_call x4 -> x6, Pallas kernels: 40.8 us -> 49.1 us  [add_inner(): pl.pallas_call(functools.partial(inner_kernel, first), grid=(size // tile...]
    slice x2 -> x5, local copies, waits for them, and re-layouts: 4.17 us -> 9.5 us  [paired(): piece = lax.slice_in_dim(a_rest, r, r + n, axis=0)]
    ppermute x6, waiting for transfers between devices: 32 us -> 36.9 us  [sum_over(): lax.ppermute(y, axis, [(i, i ^ bit) for i in range(n)])]
    ppermute x10 -> x12, starting transfers between devices: 12.7 us -> 17.5 us  [paired(): lax.ppermute(x, 'pcol', [(i, i ^ 2) for i in range(4)])]
    slice x4 -> x5, local copies, waits for them, and re-layouts: 8.25 us -> 8.05 us  [paired(): lax.slice_in_dim(u_rest, r, r + n, axis=1)]
  transfers between devices with their start and end apart: 28 -> 32, of which waited for: 14 -> 11; matrix products, arithmetic and copies ran while one was open for 4% -> 6% of each run, Pallas kernels for 22% -> 24%
where the time goes in v1:
time: 399 us; the launch traced here: 397 us
  waiting for transfers between devices  244 us (61%)
  Pallas kernels  100 us (25%)
  starting transfers between devices  29.3 us (7%)
  local copies, waits for them, and re-layouts  19.9 us (5%)
    ppermute x12, waiting for transfers between devices, paired(): lax.ppermute(x, 'pcol', [(i, i ^ 2) for i in range(4)])  207 us
    pallas_call x6, Pallas kernels, write_rows(): pl.pallas_call(update_kernel, grid=(size // tile,), in_specs=[pl.BlockSpe...  51.4 us
    pallas_call x6, Pallas kernels, add_inner(): pl.pallas_call(functools.partial(inner_kernel, first), grid=(size // tile...  49.1 us
    ppermute x6, waiting for transfers between devices, sum_over(): lax.ppermute(y, axis, [(i, i ^ bit) for i in range(n)])  36.9 us
    ppermute x12, starting transfers between devices, paired(): lax.ppermute(x, 'pcol', [(i, i ^ 2) for i in range(4)])  17.5 us
    ppermute x6, starting transfers between devices, sum_over(): lax.ppermute(y, axis, [(i, i ^ bit) for i in range(n)])  9.57 us
    slice x5, local copies, waits for them, and re-layouts, paired(): piece = lax.slice_in_dim(a_rest, r, r + n, axis=0)  9.5 us
    slice x5, local copies, waits for them, and re-layouts, paired(): lax.slice_in_dim(u_rest, r, r + n, axis=1)  8.05 us
  transfers between devices with their start and end apart: 32, of which 11 were waited for; matrix products, arithmetic and copies ran while one was open for 6% of the time, Pallas kernels for 24%

profile of v1, /device:TPU:0, one launch (start us, length us, event | category | flops | bytes accessed | tf_op | source)
XLA Modules:
  0.0 397.2 jit_solution(5431562805632221911)
XLA Ops:
  9.6 100.4 %collective-permute-done.14.refs_2_ = f32[512,128]{1,0:T(8,128)S(1)} collective-permute-done((f32[512,128]{1,0:T(8,128)S(1)}, f32[512,128]{1,0:T(8,128)S(1)}, u32[]{:S(2)}, u32[]{:S(2)}) %collective-permute-start.14) | collective-permute-done | bytes 262176 | tf_op jit(solution)/shard_map/ppermute | solution.py:133
  118.3 3.6 inner_part.6.refs_5_
  122.0 28.0 %collective-permute-done.4.refs_2_ = f32[1024,128]{1,0:T(8,128)} collective-permute-done((f32[1024,128]{1,0:T(8,128)}, f32[1024,128]{1,0:T(8,128)}, u32[]{:S(2)}, u32[]{:S(2)}) %collective-permute-start.4) | collective-permute-done | bytes 524320 | tf_op jit(solution)/shard_map/ppermute | solution.py:133
  150.6 9.4 %inner_part.7.refs_5_ = f32[512,512]{1,0:T(8,128)} custom-call(f32[12288,128]{1,0:T(8,128)} %refs_0_.17, f32[12288,128]{1,0:T(8,128)} %collective-permute-done.3.refs_1_, f32[2560,128]{1,0:T(8,128)} %collective-permute-done.12.refs_2_, f32[2560,128]{1,0:T(8,128)} %collective-permute-done.13.refs_3_, f32[12288,512]{1,0:T(8,128)} %refs_4_.11, ...), custom_call_target="tpu_custom_call" | custom-call | flops 4026531840 | bytes 10485760 | tf_op jit(solution)/shard_map/inner_part/pallas_call | solution.py:64
  160.1 10.9 %inner_part.8.refs_5_ = f32[512,512]{1,0:T(8,128)} custom-call(f32[12288,128]{1,0:T(8,128)} %refs_0_.17, f32[12288,128]{1,0:T(8,128)} %collective-permute-done.3.refs_1_, f32[3072,128]{1,0:T(8,128)} %copy-done.1, f32[3072,128]{1,0:T(8,128)} %collective-permute-done.11.refs_3_, f32[12288,512]{1,0:T(8,128)} %refs_4_.11, f32[512,512]{1,0:T(8,128)} %inner_part.7.refs_5_), custom_call_target="tpu_custom_call" | custom-call | flops 4831838208 | bytes 12582912 | tf_op jit(solution)/shard_map/inner_part/pallas_call | solution.py:64
  170.9 10.9 %inner_part.9.refs_5_ = f32[512,512]{1,0:T(8,128)} custom-call(f32[12288,128]{1,0:T(8,128)} %refs_0_.17, f32[12288,128]{1,0:T(8,128)} %collective-permute-done.3.refs_1_, f32[3072,128]{1,0:T(8,128)} %copy-done.2, f32[3072,128]{1,0:T(8,128)} %collective-permute-done.9.refs_3_, f32[12288,512]{1,0:T(8,128)} %refs_4_.11, f32[512,512]{1,0:T(8,128)} %inner_part.8.refs_5_), custom_call_target="tpu_custom_call" | custom-call | flops 4831838208 | bytes 12582912 | tf_op jit(solution)/shard_map/inner_part/pallas_call | solution.py:64
  181.8 8.1 %inner_part.10.refs_5_ = f32[512,512]{1,0:T(8,128)} custom-call(f32[12288,128]{1,0:T(8,128)} %refs_0_.17, f32[12288,128]{1,0:T(8,128)} %collective-permute-done.3.refs_1_, f32[2048,128]{1,0:T(8,128)} %collective-permute-done.6.refs_2_, f32[2048,128]{1,0:T(8,128)} %collective-permute-done.7.refs_3_, f32[12288,512]{1,0:T(8,128)} %refs_4_.11, ...), custom_call_target="tpu_custom_call" | custom-call | flops 3221225472 | bytes 8388608 | tf_op jit(solution)/shard_map/inner_part/pallas_call | solution.py:64
  190.0 6.1 %inner_part.11 = f32[512,512]{1,0:T(8,128)} custom-call(f32[12288,128]{1,0:T(8,128)} %refs_0_.17, f32[12288,128]{1,0:T(8,128)} %collective-permute-done.3.refs_1_, f32[1024,128]{1,0:T(8,128)} %collective-permute-done.4.refs_2_, f32[1024,128]{1,0:T(8,128)} %collective-permute-done.5.refs_3_, f32[12288,512]{1,0:T(8,128)} %refs_4_.11, ...), custom_call_target="tpu_custom_call" | custom-call | flops 1610612736 | bytes 4194304 | tf_op jit(solution)/shard_map/inner_part/pallas_call | solution.py:64
  199.2 3.3 fusion
  203.9 7.9 %collective-permute-done.16 = f32[256,512]{1,0:T(8,128)} collective-permute-done((f32[256,512]{1,0:T(8,128)S(1)}, f32[256,512]{1,0:T(8,128)}, u32[]{:S(2)}, u32[]{:S(2)}) %collective-permute-start.16) | collective-permute-done | bytes 524320 | tf_op jit(solution)/shard_map/ppermute | solution.py:110
  216.4 4.5 %collective-permute-done.17 = f32[128,512]{1,0:T(8,128)S(1)} collective-permute-done((f32[128,512]{1,0:T(8,128)S(1)}, f32[128,512]{1,0:T(8,128)S(1)}, u32[]{:S(2)}, u32[]{:S(2)}) %collective-permute-start.17) | collective-permute-done | bytes 262176 | tf_op jit(solution)/shard_map/ppermute | solution.py:110
  230.9 4.9 %collective-permute-done.19 = f32[64,512]{1,0:T(8,128)S(1)} collective-permute-done((f32[64,512]{1,0:T(8,128)S(1)}, f32[64,512]{1,0:T(8,128)S(1)}, u32[]{:S(2)}, u32[]{:S(2)}) %collective-permute-start.19) | collective-permute-done | bytes 131104 | tf_op jit(solution)/shard_map/ppermute | solution.py:110
  235.8 3.3 collective-permute-start.1
  240.2 66.3 %collective-permute-done.1.refs_2_ = f32[128,512]{1,0:T(8,128)S(1)} collective-permute-done((f32[128,512]{1,0:T(8,128)S(1)}, f32[128,512]{1,0:T(8,128)S(1)}, u32[]{:S(2)}, u32[]{:S(2)}) %collective-permute-start.1) | collective-permute-done | bytes 262176 | tf_op jit(solution)/shard_map/ppermute | solution.py:133
  311.1 5.8 %collective-permute-done.20 = f32[128,512]{1,0:T(8,128)S(1)} collective-permute-done((f32[128,512]{1,0:T(8,128)S(1)}, f32[128,512]{1,0:T(8,128)S(1)}, u32[]{:S(2)}, u32[]{:S(2)}) %collective-permute-start.20) | collective-permute-done | bytes 262176 | tf_op jit(solution)/shard_map/ppermute | solution.py:110
  316.9 2.9 collective-permute-done.22.refs_2_
  322.0 11.4 %collective-permute-done.21 = f32[256,512]{1,0:T(8,128)S(1)} collective-permute-done((f32[256,512]{1,0:T(8,128)S(1)}, f32[256,512]{1,0:T(8,128)S(1)}, u32[]{:S(2)}, u32[]{:S(2)}) %collective-permute-start.21) | collective-permute-done | bytes 524320 | tf_op jit(solution)/shard_map/ppermute | solution.py:110
  334.5 8.9 %collective-permute-done.24.refs_2_ = f32[128,2048]{1,0:T(8,128)} collective-permute-done((f32[128,2048]{1,0:T(8,128)S(1)}, f32[128,2048]{1,0:T(8,128)}, u32[]{:S(2)}, u32[]{:S(2)}) %collective-permute-start.24) | collective-permute-done | bytes 1048608 | tf_op jit(solution)/shard_map/ppermute | solution.py:133
  344.6 11.4 %update_rows.6.refs_6_ = f32[12288,512]{1,0:T(8,128)} custom-call(f32[128,12288]{1,0:T(8,128)} %refs_0_.23, f32[128,12288]{1,0:T(8,128)} %collective-permute-done.refs_1_, f32[128,3072]{1,0:T(8,128)} %collective-permute-done.30.refs_2_, f32[128,3072]{1,0:T(8,128)} %copy-done.3, f32[512,512]{1,0:T(8,128)} %pad_maximum_fusion.refs_4_, f32[12288,512]{1,0:T(8,128)} %refs_5_.11, ...), custom_call_target="tpu_custom_call" | custom-call | flops 4831838208 | bytes 18874368 | tf_op jit(solution)/shard_map/update_rows/pallas_call | solution.py:86
  357.2 11.4 %update_rows.7.refs_6_ = f32[12288,512]{1,0:T(8,128)} custom-call(f32[128,12288]{1,0:T(8,128)} %refs_0_.23, f32[128,12288]{1,0:T(8,128)} %collective-permute-done.refs_1_, f32[128,3072]{1,0:T(8,128)} %collective-permute-done.28.refs_2_, f32[128,3072]{1,0:T(8,128)} %copy-done.4, f32[512,512]{1,0:T(8,128)} %pad_maximum_fusion.refs_4_, ...), custom_call_target="tpu_custom_call", output_to_operand_aliasing={{}: (6, {})} | custom-call | flops 4831838208 | bytes 18874368 | tf_op jit(solution)/shard_map/update_rows/pallas_call | solution.py:86
  368.6 10.1 %update_rows.8.refs_6_ = f32[12288,512]{1,0:T(8,128)} custom-call(f32[128,12288]{1,0:T(8,128)} %refs_0_.23, f32[128,12288]{1,0:T(8,128)} %collective-permute-done.refs_1_, f32[128,2560]{1,0:T(8,128)} %collective-permute-done.26.refs_2_, f32[128,2560]{1,0:T(8,128)} %collective-permute-done.27.refs_3_, ...), custom_call_target="tpu_custom_call", output_to_operand_aliasing={{}: (6, {})} | custom-call | flops 4026531840 | bytes 15728640 | tf_op jit(solution)/shard_map/update_rows/pallas_call | solution.py:86
  378.8 8.4 %update_rows.9.refs_6_ = f32[12288,512]{1,0:T(8,128)} custom-call(f32[128,12288]{1,0:T(8,128)} %refs_0_.23, f32[128,12288]{1,0:T(8,128)} %collective-permute-done.refs_1_, f32[128,2048]{1,0:T(8,128)} %collective-permute-done.24.refs_2_, f32[128,2048]{1,0:T(8,128)} %collective-permute-done.25.refs_3_, ...), custom_call_target="tpu_custom_call", output_to_operand_aliasing={{}: (6, {})} | custom-call | flops 3221225472 | bytes 12582912 | tf_op jit(solution)/shard_map/update_rows/pallas_call | solution.py:86
  387.1 6.1 %update_rows.10.refs_6_ = f32[12288,512]{1,0:T(8,128)} custom-call(f32[128,12288]{1,0:T(8,128)} %refs_0_.23, f32[128,12288]{1,0:T(8,128)} %collective-permute-done.refs_1_, f32[128,1024]{1,0:T(8,128)} %collective-permute-done.22.refs_2_, f32[128,1024]{1,0:T(8,128)} %collective-permute-done.23.refs_3_, ...), custom_call_target="tpu_custom_call", output_to_operand_aliasing={{}: (6, {})} | custom-call | flops 1610612736 | bytes 6291456 | tf_op jit(solution)/shard_map/update_rows/pallas_call | solution.py:86
  393.2 4.0 update_rows.11
  (91 shorter events, 48.9 us)
Async XLA Ops:
  0.0 117.4 %collective-permute-start.3 = (f32[12288,128]{1,0:T(8,128)}, f32[12288,128]{1,0:T(8,128)}, u32[]{:S(2)}, u32[]{:S(2)}) collective-permute-start(f32[12288,128]{1,0:T(8,128)} %refs_0_.17), channel_id=1, source_target_pairs={{0,1},{1,0},{2,3},{3,2},{4,5},{5,4},{6,7},{7,6},{8,9},{9,8},{10,11... | collective-permute-start | bytes 18874376 | tf_op jit(solution)/shard_map/ppermute | solution.py:132
  5.0 105.5 %collective-permute-start.10 = (f32[3072,128]{1,0:T(8,128)S(1)}, f32[3072,128]{1,0:T(8,128)S(1)}, u32[]{:S(2)}, u32[]{:S(2)}) collective-permute-start(f32[3072,128]{1,0:T(8,128)S(1)} %get-tuple-element.19), channel_id=1, source_target_pairs={{0,2},{1,3},{2,0},{3,1},{4,6},{5,7},{6,4},{7,5},{8,10},{9,11},{10,... | collective-permute-start | bytes 4718600 | tf_op jit(solution)/shard_map/ppermute | solution.py:133
  7.5 102.5 %collective-permute-start.12 = (f32[2560,128]{1,0:T(8,128)S(1)}, f32[2560,128]{1,0:T(8,128)}, u32[]{:S(2)}, u32[]{:S(2)}) collective-permute-start(f32[2560,128]{1,0:T(8,128)S(1)} %slice.55), channel_id=1, source_target_pairs={{0,2},{1,3},{2,0},{3,1},{4,6},{5,7},{6,4},{7,5},{8,10},{9,11},{10,... | collective-permute-start | bytes 3932168 | tf_op jit(solution)/shard_map/ppermute | solution.py:133
  7.6 107.5 %collective-permute-start.8 = (f32[3072,128]{1,0:T(8,128)S(1)}, f32[3072,128]{1,0:T(8,128)S(1)}, u32[]{:S(2)}, u32[]{:S(2)}) collective-permute-start(f32[3072,128]{1,0:T(8,128)S(1)} %get-tuple-element.20), channel_id=1, source_target_pairs={{0,2},{1,3},{2,0},{3,1},{4,6},{5,7},{6,4},{7,5},{8,10},{9,11},{10,... | collective-permute-start | bytes 4718600 | tf_op jit(solution)/shard_map/ppermute | solution.py:133
  9.5 100.5 %collective-permute-start.14 = (f32[512,128]{1,0:T(8,128)S(1)}, f32[512,128]{1,0:T(8,128)S(1)}, u32[]{:S(2)}, u32[]{:S(2)}) collective-permute-start(f32[512,128]{1,0:T(8,128)S(1)} %slice.54), channel_id=1, source_target_pairs={{0,2},{1,3},{2,0},{3,1},{4,6},{5,7},{6,4},{7,5},{8,10},{9,11},{10,... | collective-permute-start | bytes 786440 | tf_op jit(solution)/shard_map/ppermute | solution.py:133
  110.0 40.6 %collective-permute-start.13 = (f32[2560,128]{1,0:T(8,128)}, f32[2560,128]{1,0:T(8,128)}, u32[]{:S(2)}, u32[]{:S(2)}) collective-permute-start(f32[2560,128]{1,0:T(8,128)} %collective-permute-done.12.refs_2_), channel_id=1, source_target_pairs={{0,1},{1,0},{2,3},{3,2},{4,5},{5,4},{6,7},{7,6},{8,9},{9,8},{10,11... | collective-permute-start | bytes 3932168 | tf_op jit(solution)/shard_map/ppermute | solution.py:132
  110.5 49.5 %collective-permute-start.11 = (f32[3072,128]{1,0:T(8,128)S(1)}, f32[3072,128]{1,0:T(8,128)}, u32[]{:S(2)}, u32[]{:S(2)}) collective-permute-start(f32[3072,128]{1,0:T(8,128)S(1)} %collective-permute-done.10.refs_2_), channel_id=1, source_target_pairs={{0,1},{1,0},{2,3},{3,2},{4,5},{5,4},{6,7},{7,6},{8,9},{9,8},{10,11... | collective-permute-start | bytes 4718600 | tf_op jit(solution)/shard_map/ppermute | solution.py:132
  113.4 36.7 %collective-permute-start.6 = (f32[2048,128]{1,0:T(8,128)}, f32[2048,128]{1,0:T(8,128)}, u32[]{:S(2)}, u32[]{:S(2)}) collective-permute-start(f32[2048,128]{1,0:T(8,128)} %slice.58), channel_id=1, source_target_pairs={{0,2},{1,3},{2,0},{3,1},{4,6},{5,7},{6,4},{7,5},{8,10},{9,11},{10,... | collective-permute-start | bytes 3145736 | tf_op jit(solution)/shard_map/ppermute | solution.py:133
  115.1 55.8 %collective-permute-start.9 = (f32[3072,128]{1,0:T(8,128)S(1)}, f32[3072,128]{1,0:T(8,128)}, u32[]{:S(2)}, u32[]{:S(2)}) collective-permute-start(f32[3072,128]{1,0:T(8,128)S(1)} %collective-permute-done.8.refs_2_), channel_id=1, source_target_pairs={{0,1},{1,0},{2,3},{3,2},{4,5},{5,4},{6,7},{7,6},{8,9},{9,8},{10,11... | collective-permute-start | bytes 4718600 | tf_op jit(solution)/shard_map/ppermute | solution.py:132
  117.4 32.6 %collective-permute-start.4 = (f32[1024,128]{1,0:T(8,128)}, f32[1024,128]{1,0:T(8,128)}, u32[]{:S(2)}, u32[]{:S(2)}) collective-permute-start(f32[1024,128]{1,0:T(8,128)} %slice.57), channel_id=1, source_target_pairs={{0,2},{1,3},{2,0},{3,1},{4,6},{5,7},{6,4},{7,5},{8,10},{9,11},{10,... | collective-permute-start | bytes 1572872 | tf_op jit(solution)/shard_map/ppermute | solution.py:133
  150.0 193.9 %collective-permute-start = (f32[128,12288]{1,0:T(8,128)}, f32[128,12288]{1,0:T(8,128)}, u32[]{:S(2)}, u32[]{:S(2)}) collective-permute-start(f32[128,12288]{1,0:T(8,128)} %refs_0_.23), channel_id=1, source_target_pairs={{0,1},{1,0},{2,3},{3,2},{4,5},{5,4},{6,7},{7,6},{8,9},{9,8},{10,11... | collective-permute-start | bytes 18874376 | tf_op jit(solution)/shard_map/ppermute | solution.py:132
  150.0 39.9 %collective-permute-start.5 = (f32[1024,128]{1,0:T(8,128)}, f32[1024,128]{1,0:T(8,128)}, u32[]{:S(2)}, u32[]{:S(2)}) collective-permute-start(f32[1024,128]{1,0:T(8,128)} %collective-permute-done.4.refs_2_), channel_id=1, source_target_pairs={{0,1},{1,0},{2,3},{3,2},{4,5},{5,4},{6,7},{7,6},{8,9},{9,8},{10,11... | collective-permute-start | bytes 1572872 | tf_op jit(solution)/shard_map/ppermute | solution.py:132
  150.6 31.2 %collective-permute-start.7 = (f32[2048,128]{1,0:T(8,128)}, f32[2048,128]{1,0:T(8,128)}, u32[]{:S(2)}, u32[]{:S(2)}) collective-permute-start(f32[2048,128]{1,0:T(8,128)} %collective-permute-done.6.refs_2_), channel_id=1, source_target_pairs={{0,1},{1,0},{2,3},{3,2},{4,5},{5,4},{6,7},{7,6},{8,9},{9,8},{10,11... | collective-permute-start | bytes 3145736 | tf_op jit(solution)/shard_map/ppermute | solution.py:132
  202.5 105.6 %collective-permute-start.30 = (f32[128,3072]{1,0:T(8,128)}, f32[128,3072]{1,0:T(8,128)}, u32[]{:S(2)}, u32[]{:S(2)}) collective-permute-start(f32[128,3072]{1,0:T(8,128)} %get-tuple-element.17), channel_id=1, source_target_pairs={{0,2},{1,3},{2,0},{3,1},{4,6},{5,7},{6,4},{7,5},{8,10},{9,11},{10,... | collective-permute-start | bytes 4718600 | tf_op jit(solution)/shard_map/ppermute | solution.py:133
  214.9 93.2 %collective-permute-start.28 = (f32[128,3072]{1,0:T(8,128)S(1)}, f32[128,3072]{1,0:T(8,128)}, u32[]{:S(2)}, u32[]{:S(2)}) collective-permute-start(f32[128,3072]{1,0:T(8,128)S(1)} %get-tuple-element.18), channel_id=1, source_target_pairs={{0,2},{1,3},{2,0},{3,1},{4,6},{5,7},{6,4},{7,5},{8,10},{9,11},{10,... | collective-permute-start | bytes 4718600 | tf_op jit(solution)/shard_map/ppermute | solution.py:133
  225.3 96.0 %collective-permute-start.26 = (f32[128,2560]{1,0:T(8,128)S(1)}, f32[128,2560]{1,0:T(8,128)}, u32[]{:S(2)}, u32[]{:S(2)}) collective-permute-start(f32[128,2560]{1,0:T(8,128)S(1)} %slice.69), channel_id=1, source_target_pairs={{0,2},{1,3},{2,0},{3,1},{4,6},{5,7},{6,4},{7,5},{8,10},{9,11},{10,... | collective-permute-start | bytes 3932168 | tf_op jit(solution)/shard_map/ppermute | solution.py:133
  235.8 70.7 %collective-permute-start.1 = (f32[128,512]{1,0:T(8,128)S(1)}, f32[128,512]{1,0:T(8,128)S(1)}, u32[]{:S(2)}, u32[]{:S(2)}) collective-permute-start(f32[128,512]{1,0:T(8,128)S(1)} %slice.56), channel_id=1, source_target_pairs={{0,2},{1,3},{2,0},{3,1},{4,6},{5,7},{6,4},{7,5},{8,10},{9,11},{10,... | collective-permute-start | bytes 786440 | tf_op jit(solution)/shard_map/ppermute | solution.py:133
  308.0 35.4 %collective-permute-start.31 = (f32[128,3072]{1,0:T(8,128)}, f32[128,3072]{1,0:T(8,128)S(1)}, u32[]{:S(2)}, u32[]{:S(2)}) collective-permute-start(f32[128,3072]{1,0:T(8,128)} %collective-permute-done.30.refs_2_), channel_id=1, source_target_pairs={{0,1},{1,0},{2,3},{3,2},{4,5},{5,4},{6,7},{7,6},{8,9},{9,8},{10,11... | collective-permute-start | bytes 4718600 | tf_op jit(solution)/shard_map/ppermute | solution.py:132
  316.9 39.1 %collective-permute-start.29 = (f32[128,3072]{1,0:T(8,128)}, f32[128,3072]{1,0:T(8,128)S(1)}, u32[]{:S(2)}, u32[]{:S(2)}) collective-permute-start(f32[128,3072]{1,0:T(8,128)} %collective-permute-done.28.refs_2_), channel_id=1, source_target_pairs={{0,1},{1,0},{2,3},{3,2},{4,5},{5,4},{6,7},{7,6},{8,9},{9,8},{10,11... | collective-permute-start | bytes 4718600 | tf_op jit(solution)/shard_map/ppermute | solution.py:132
  319.8 23.6 %collective-permute-start.24 = (f32[128,2048]{1,0:T(8,128)S(1)}, f32[128,2048]{1,0:T(8,128)}, u32[]{:S(2)}, u32[]{:S(2)}) collective-permute-start(f32[128,2048]{1,0:T(8,128)S(1)} %slice.68), channel_id=1, source_target_pairs={{0,2},{1,3},{2,0},{3,1},{4,6},{5,7},{6,4},{7,5},{8,10},{9,11},{10,... | collective-permute-start | bytes 3145736 | tf_op jit(solution)/shard_map/ppermute | solution.py:133
  333.4 35.2 %collective-permute-start.27 = (f32[128,2560]{1,0:T(8,128)}, f32[128,2560]{1,0:T(8,128)}, u32[]{:S(2)}, u32[]{:S(2)}) collective-permute-start(f32[128,2560]{1,0:T(8,128)} %collective-permute-done.26.refs_2_), channel_id=1, source_target_pairs={{0,1},{1,0},{2,3},{3,2},{4,5},{5,4},{6,7},{7,6},{8,9},{9,8},{10,11... | collective-permute-start | bytes 3932168 | tf_op jit(solution)/shard_map/ppermute | solution.py:132
  343.4 49.8 %collective-permute-start.2 = (f32[128,512]{1,0:T(8,128)S(1)}, f32[128,512]{1,0:T(8,128)}, u32[]{:S(2)}, u32[]{:S(2)}) collective-permute-start(f32[128,512]{1,0:T(8,128)S(1)} %collective-permute-done.1.refs_2_), channel_id=1, source_target_pairs={{0,1},{1,0},{2,3},{3,2},{4,5},{5,4},{6,7},{7,6},{8,9},{9,8},{10,11... | collective-permute-start | bytes 786440 | tf_op jit(solution)/shard_map/ppermute | solution.py:132
  343.5 43.7 %collective-permute-start.23 = (f32[128,1024]{1,0:T(8,128)}, f32[128,1024]{1,0:T(8,128)}, u32[]{:S(2)}, u32[]{:S(2)}) collective-permute-start(f32[128,1024]{1,0:T(8,128)} %collective-permute-done.22.refs_2_), channel_id=1, source_target_pairs={{0,1},{1,0},{2,3},{3,2},{4,5},{5,4},{6,7},{7,6},{8,9},{9,8},{10,11... | collective-permute-start | bytes 1572872 | tf_op jit(solution)/shard_map/ppermute | solution.py:132
  344.0 34.8 %collective-permute-start.25 = (f32[128,2048]{1,0:T(8,128)}, f32[128,2048]{1,0:T(8,128)}, u32[]{:S(2)}, u32[]{:S(2)}) collective-permute-start(f32[128,2048]{1,0:T(8,128)} %collective-permute-done.24.refs_2_), channel_id=1, source_target_pairs={{0,1},{1,0},{2,3},{3,2},{4,5},{5,4},{6,7},{7,6},{8,9},{9,8},{10,11... | collective-permute-start | bytes 3145736 | tf_op jit(solution)/shard_map/ppermute | solution.py:132
  (16 other events, 153.5 us)
